TPU v7x, 512 devices: a whole 4x8x8 slice. The times are simulated.
512 devices in a mesh: grid: 16 (over y, core), dom: 32 (over z, x).
Axes of the slice: x: 4, y: 8, z: 8, core: 2. Of those that a mesh axis runs over, the one named last changes fastest.
Arguments:
- state: float32 [5, 125, 65536], P(None, None, ('grid', 'dom')), as said below
- inv_size: float32 [3, 65536], P(None, ('grid', 'dom')), may hold values from 1 to 4
- plus_order: int32 [3, 65536], P(None, ('grid', 'dom')), may hold values from 0 to 127, as said below
- minus_order: int32 [3, 65536], P(None, ('grid', 'dom')), may hold values from 0 to 127, as said below
- donor_cell: int32 [512, 1024], P(('grid', 'dom')), may hold values from 0 to 127
- donor_weights: float32 [512, 3, 5, 1024], P(('grid', 'dom')), as said below
- recv_slot: int32 [512, 600], P(('grid', 'dom')), may hold values from 0 to 1023, as said below
Outputs:
- rhs: float32 [5, 125, 65536], P(None, None, ('grid', 'dom'))
Inputs may be any that keep to these rules, and one draw needn't show every extreme that they name: `plus_order`: within each device's block of 128 columns, every row is a permutation of the local element numbers. `minus_order`: within each device's block of 128 columns, every row is a permutation of the local element numbers. `state`: density lies in [0.9, 1.1], each momentum in [-0.1, 0.1], energy in [2.4, 2.6]. `donor_weights`: for each donor device, direction and slot, the five weights are the Lagrange basis of the five Gauss-Legendre points evaluated at one coordinate in [-0.8, 0.8]. `recv_slot`: entries of one device's row are distinct, and each names a slot whose source device (the slot // 2) lies in another grid than the row's device.
All inputs are finite; a program needn't handle non-finite values.
Results may differ from a plain program's by a relative error of at most 0.0003.
Values sent between devices are 32-bit elements; how exact they have to be, the bound alone decides.
A program may use at most 64 MiB of HBM per device.

v0:
```python
import math
import jax
import jax.numpy as jnp
from jax import lax
from jax.sharding import PartitionSpec as P

precise = lax.Precision.HIGHEST
volume_forms = ("ia,vabce->vibce", "ib,vabce->vaice", "ic,vabce->vabie")
face_forms = ("a,vabce->vbce", "b,vabce->vace", "c,vabce->vabe")
lift_forms = ("i,vbce->vibce", "i,vace->vaice", "i,vabe->vabie")


def gauss_nodes():
    outer = math.sqrt(5.0 + 2.0 * math.sqrt(10.0 / 7.0)) / 3.0
    inner = math.sqrt(5.0 - 2.0 * math.sqrt(10.0 / 7.0)) / 3.0
    return [-outer, -inner, 0.0, inner, outer]


def basis_value(nodes, column, target_positions):
    value = 1.0
    for other in range(5):
        if other != column:
            value = value * (target_positions - nodes[other]) / (nodes[column] - nodes[other])
    return value


def basis_slope(nodes, column, target_positions):
    total = 0.0
    for skipped in range(5):
        if skipped != column:
            value = 1.0 / (nodes[column] - nodes[skipped])
            for other in range(5):
                if other != column and other != skipped:
                    value = (
                        value * (target_positions - nodes[other]) / (nodes[column] - nodes[other])
                    )
            total = total + value
    return total


def legendre_slopes(target_positions):
    values = [1.0, target_positions]
    slopes = [0.0, 1.0]
    for order in range(1, 5):
        values.append(
            ((2 * order + 1) * target_positions * values[order] - order * values[order - 1])
            / (order + 1)
        )
        slopes.append(slopes[order - 1] + (2 * order + 1) * values[order])
    return (slopes[4], slopes[5])


def tables():
    nodes = gauss_nodes()
    deriv = [[basis_slope(nodes, column, nodes[row]) for column in range(5)] for row in range(5)]
    lower = [basis_value(nodes, column, -1.0) for column in range(5)]
    upper = [basis_value(nodes, column, 1.0) for column in range(5)]
    lift_low = []
    lift_high = []
    for row in range(5):
        slope_four, slope_five = legendre_slopes(nodes[row])
        lift_low.append(-0.5 * (slope_five - slope_four))
        lift_high.append(0.5 * (slope_five + slope_four))
    return tuple(
        (jnp.asarray(matrix, jnp.float32) for matrix in (deriv, lower, upper, lift_low, lift_high))
    )


def euler_flux(state, direction):
    density = state[0]
    momenta = state[1:4]
    energy = state[4]
    speed = momenta[direction] / density
    pressure = 0.4 * (energy - 0.5 * jnp.sum(momenta * momenta, axis=0) / density)
    pieces = [
        momenta[direction],
        momenta[0] * speed,
        momenta[1] * speed,
        momenta[2] * speed,
        (energy + pressure) * speed,
    ]
    pieces[1 + direction] = pieces[1 + direction] + pressure
    sound = jnp.sqrt(1.4 * pressure / density)
    return (jnp.stack(pieces), jnp.abs(speed) + sound)


def common_flux(left_state, right_state, direction):
    left_flux, left_wave = euler_flux(left_state, direction)
    right_flux, right_wave = euler_flux(right_state, direction)
    wave = jnp.maximum(left_wave, right_wave)
    return 0.5 * (left_flux + right_flux) - 0.5 * wave * (right_state - left_state)


def remote_fluxes(left_states, right_states):
    return jnp.stack(
        [
            common_flux(left_states[direction], right_states[direction], direction)
            for direction in range(3)
        ]
    )


def slot_states(state, plus_rows, minus_rows):
    deriv, lower, upper, lift_low, lift_high = tables()
    columns = state.shape[-1]
    grid_form = state.reshape(5, 5, 5, 5, columns)
    high_slots = []
    low_slots = []
    for direction in range(3):
        high_face = jnp.einsum(face_forms[direction], upper, grid_form, precision=precise).reshape(
            5, 25, columns
        )
        low_face = jnp.einsum(face_forms[direction], lower, grid_form, precision=precise).reshape(
            5, 25, columns
        )
        high_slots.append(jnp.take(high_face, plus_rows[direction], axis=2))
        low_slots.append(jnp.take(low_face, minus_rows[direction], axis=2))
    return (jnp.stack(high_slots), jnp.stack(low_slots))


def interpolate(state, cells, weights, blocks):
    block_width = cells.shape[0] // blocks

    def one_block(index):
        block_cells = lax.dynamic_slice_in_dim(cells, index * block_width, block_width)
        block_weights = lax.dynamic_slice_in_dim(weights, index * block_width, block_width, axis=2)
        gathered = jnp.take(state, block_cells, axis=2).reshape(5, 5, 5, 5, block_width)
        reduced = jnp.einsum("as,vabcs->vbcs", block_weights[0], gathered, precision=precise)
        reduced = jnp.einsum("bs,vbcs->vcs", block_weights[1], reduced, precision=precise)
        return jnp.einsum("cs,vcs->vs", block_weights[2], reduced, precision=precise)

    values = lax.map(one_block, jnp.arange(blocks, dtype=jnp.int32))
    return jnp.transpose(values, (1, 0, 2)).reshape(5, blocks * block_width)


def inverse_order(rows):
    count = rows.shape[0]
    return jnp.zeros((count,), jnp.int32).at[rows].set(jnp.arange(count, dtype=jnp.int32))


def assemble(high_slots, low_slots, remote_plus, remote_minus, fringe, plus_rows, minus_rows):
    remote = remote_plus.shape[-1]
    start = remote + fringe.shape[-1]
    plus_parts = []
    minus_parts = []
    for direction in range(3):
        local_flux = common_flux(
            high_slots[direction][:, :, start:], low_slots[direction][:, :, start:], direction
        )
        fringe_high = common_flux(
            high_slots[direction][:, :, remote:start], fringe[direction, 1], direction
        )
        fringe_low = common_flux(
            fringe[direction, 0], low_slots[direction][:, :, remote:start], direction
        )
        plus_slots = jnp.concatenate([remote_plus[direction], fringe_high, local_flux], axis=2)
        minus_slots = jnp.concatenate([remote_minus[direction], fringe_low, local_flux], axis=2)
        plus_parts.append(jnp.take(plus_slots, inverse_order(plus_rows[direction]), axis=2))
        minus_parts.append(jnp.take(minus_slots, inverse_order(minus_rows[direction]), axis=2))
    return (jnp.stack(plus_parts), jnp.stack(minus_parts))


def divergence(state, scales, plus_common, minus_common):
    deriv, lower, upper, lift_low, lift_high = tables()
    columns = state.shape[-1]
    grid_form = state.reshape(5, 5, 5, 5, columns)
    total = jnp.zeros_like(grid_form)
    for direction in range(3):
        flux = euler_flux(grid_form, direction)[0]
        inner = jnp.einsum(volume_forms[direction], deriv, flux, precision=precise)
        low_jump = minus_common[direction].reshape(5, 5, 5, columns) - jnp.einsum(
            face_forms[direction], lower, flux, precision=precise
        )
        high_jump = plus_common[direction].reshape(5, 5, 5, columns) - jnp.einsum(
            face_forms[direction], upper, flux, precision=precise
        )
        inner = inner + jnp.einsum(lift_forms[direction], lift_low, low_jump, precision=precise)
        inner = inner + jnp.einsum(lift_forms[direction], lift_high, high_jump, precision=precise)
        total = total + scales[direction] * inner
    return (-total).reshape(5, 125, columns)


def body(state, inv_size, plus_order, minus_order, donor_cell, donor_weights, recv_slot):
    columns = state.shape[-1]
    part_count = lax.axis_size("dom")
    grid_count = lax.axis_size("grid")
    capacity = max(1, columns // (3 * part_count))
    remote = part_count * capacity
    fringe_count = recv_slot.shape[-1] // 150
    high_slots, low_slots = slot_states(state, plus_order, minus_order)
    values = interpolate(state, donor_cell[0], donor_weights[0], grid_count)
    slot_count = values.shape[1] // (grid_count * part_count)
    shaped = values.reshape(5, grid_count, part_count, slot_count)
    arrived = lax.all_to_all(
        lax.all_to_all(shaped, "grid", split_axis=1, concat_axis=1, tiled=True),
        "dom",
        split_axis=2,
        concat_axis=2,
        tiled=True,
    )
    arrived = arrived.reshape(5, grid_count * part_count * slot_count)
    fringe = jnp.take(arrived, recv_slot[0], axis=1)
    fringe = jnp.transpose(fringe.reshape(5, 3, 2, 25, fringe_count), (1, 2, 0, 3, 4))
    own_high = high_slots[..., :remote]
    own_low = low_slots[..., :remote]
    outgoing = own_low.reshape(3, 5, 25, part_count, capacity)
    partner_low = lax.all_to_all(outgoing, "dom", split_axis=3, concat_axis=3, tiled=True).reshape(
        3, 5, 25, remote
    )
    remote_plus = remote_fluxes(own_high, partner_low)
    returned = lax.all_to_all(
        remote_plus.reshape(3, 5, 25, part_count, capacity),
        "dom",
        split_axis=3,
        concat_axis=3,
        tiled=True,
    )
    remote_minus = returned.reshape(3, 5, 25, remote)
    plus_common, minus_common = assemble(
        high_slots, low_slots, remote_plus, remote_minus, fringe, plus_order, minus_order
    )
    return divergence(state, inv_size, plus_common, minus_common)


def solution(mesh):
    return jax.shard_map(
        body,
        mesh=mesh,
        in_specs=(
            P(None, None, ("grid", "dom")),
            P(None, ("grid", "dom")),
            P(None, ("grid", "dom")),
            P(None, ("grid", "dom")),
            P(("grid", "dom"), None),
            P(("grid", "dom"), None, None, None),
            P(("grid", "dom"), None),
        ),
        out_specs=P(None, None, ("grid", "dom")),
        check_vma=False,
    )
```

profile of v0, /device:TPU:8, one launch (start us, length us, event | category | flops | bytes accessed | tf_op | source)
XLA Modules:
  0.0 255.1 jit_solution(12432255003614025478)
XLA Ops:
  0.0 1.2 copy.2740
  1.3 58.2 %while.10 = (s32[]{:T(128)}, f32[16,5,64]{2,1,0:T(8,128)S(1)}, s32[16]{0:T(128)S(1)}, s32[1024]{0:T(1024)}, f32[5,125,128]{1,0,2:T(8,128)S(1)}, /*index=5*/f32[3...) while((s32[]{:T(128)}, f32[16,5,64]{2,1,0:T(8,128)S(1)}, ...), condition=%wide.region_8.10_spmd, body=%wide.region_7.9_spmd.sunk | while | flops 130696 | bytes 1246307 | solution.py:132
  60.5 9.6 %all-to-all-start.2 = ((f32[16,1,320]{2,1,0:T(1,128)}), f32[16,1,320]{2,1,0:T(1,128)}, u32[]{:S(2)}, u32[]{:S(2)}) async-start(f32[16,1,320]{2,1,0:T(1,128)} %reshape.3685), calls=%async_computation.2 | async-start | bytes 49152 | tf_op jit(solution)/shard_map/all_to_all | solution.py:195
  76.0 0.9 fusion.35
  78.8 1.2 fusion.220
  84.0 1.2 fusion.221
  95.3 1.0 scatter_custom_fusion
  98.5 0.9 fusion.36
  102.5 1.0 scatter_custom_fusion.3
  104.7 1.0 scatter_custom_fusion.2
  106.7 1.2 scatter_custom_fusion.1
  111.9 1.2 fusion.224
  113.1 1.2 fusion.20
  114.3 1.2 fusion.18
  115.5 1.2 fusion.225
  116.7 1.0 copy.2844
  118.3 2.5 gather_fusion.5
  121.4 1.9 fusion.39
  126.7 1.2 scatter_custom_fusion.5
  129.1 1.4 fusion.22
  130.4 1.4 fusion.16
  131.9 1.2 fusion.12
  133.1 1.1 scatter_custom_fusion.4
  135.3 1.2 fusion.14
  147.7 0.8 copy-done.60
  160.0 0.9 copy-done.32
  160.9 1.7 fusion.30
  164.5 1.4 reduce.22
  167.1 11.6 %all-to-all-start.3 = ((f32[32,1,160]{2,1,0:T(1,128)}), f32[32,1,160]{2,1,0:T(1,128)}, u32[]{:S(2)}, u32[]{:S(2)}) async-start(f32[32,1,160]{2,1,0:T(1,128)} %reshape.3687), calls=%async_computation.3 | async-start | bytes 65536 | tf_op jit(solution)/shard_map/all_to_all | solution.py:194
  180.3 1.3 reduce.24
  181.6 0.8 reshape.3689
  183.5 4.7 %all-to-all-done.3 = f32[32,1,160]{2,1,0:T(1,128)} async-done(((f32[32,1,160]{2,1,0:T(1,128)}), f32[32,1,160]{2,1,0:T(1,128)}, u32[]{:S(2)}, u32[]{:S(2)}) %all-to-all-start.3) | async-done | bytes 20512 | tf_op jit(solution)/shard_map/all_to_all | solution.py:194
  188.2 4.9 %all-to-all-start = ((f32[32,1,375]{2,1,0:T(1,128)}), f32[32,1,375]{2,1,0:T(1,128)}, u32[]{:S(2)}, u32[]{:S(2)}) async-start(f32[32,1,375]{2,1,0:T(1,128)} %reshape.3689), calls=%async_computation | async-start | bytes 98304 | tf_op jit(solution)/shard_map/all_to_all | solution.py:207
  193.1 1.5 reduce.23
  194.6 0.8 reshape.3688
  195.4 1.8 copy.2745
  197.2 2.3 gather_fusion.1
  199.4 1.2 copy.2747
  204.1 1.5 reduce.25
  208.6 0.9 copy-done.71
  209.5 0.9 copy-done.65
  210.7 1.3 reduce.26
  211.9 0.8 reshape.3691
  212.7 10.0 %all-to-all-start.1 = ((f32[32,1,375]{2,1,0:T(1,128)}), f32[32,1,375]{2,1,0:T(1,128)S(1)}, u32[]{:S(2)}, u32[]{:S(2)}) async-start(f32[32,1,375]{2,1,0:T(1,128)} %reshape.3691), calls=%async_computation.1 | async-start | bytes 98304 | tf_op jit(solution)/shard_map/all_to_all | solution.py:211
  222.8 0.8 copy-done.62
  223.7 0.9 copy-done.59
  224.6 0.9 copy-done.68
  226.1 6.2 %all-to-all-done.1 = f32[32,1,375]{2,1,0:T(1,128)S(1)} async-done(((f32[32,1,375]{2,1,0:T(1,128)}), f32[32,1,375]{2,1,0:T(1,128)S(1)}, u32[]{:S(2)}, u32[]{:S(2)}) %all-to-all-start.1) | async-done | bytes 48032 | tf_op jit(solution)/shard_map/all_to_all | solution.py:211
  234.7 0.9 gather_fusion.8
  236.0 0.8 copy-done.47
  236.9 0.9 copy-done.14
  238.0 0.9 gather_fusion.11
  239.4 0.8 copy-done.46
  240.4 0.9 gather_fusion.10
  241.8 0.8 copy-done.45
  242.8 0.9 gather_fusion.9
  244.2 0.8 copy-done.43
  245.0 0.8 copy-done.34
  245.9 0.9 copy-done.33
  247.1 0.9 gather_fusion.13
  248.4 0.8 copy-done.44
  249.5 0.9 gather_fusion.12
  250.8 0.8 copy-done.42
  253.4 0.8 fusion.6
  (825 shorter events, 131.7 us)
Async XLA Ops:
  0.0 1.2 copy-start.92
  59.5 10.6 %copy-start = (f32[5,125,128]{2,1,0:T(8,128)S(1)}, f32[5,125,128]{2,1,0:T(8,128)}, u32[]{:S(2)}) copy-start(f32[5,125,128]{2,1,0:T(8,128)} %param.18) | copy-start | bytes 960004
  60.5 103.5 %all-to-all-start.2 = ((f32[16,1,320]{2,1,0:T(1,128)}), f32[16,1,320]{2,1,0:T(1,128)}, u32[]{:S(2)}, u32[]{:S(2)}) async-start(f32[16,1,320]{2,1,0:T(1,128)} %reshape.3685), calls=%async_computation.2 | async-start | bytes 49152 | tf_op jit(solution)/shard_map/all_to_all | solution.py:195
  92.9 4.6 %copy-start.41 = (f32[1,5,25,128]{3,0,2,1:T(1,128)S(1)}, f32[1,5,25,128]{3,0,2,1:T(1,128)}, u32[]{:S(2)}) copy-start(f32[1,5,25,128]{3,0,2,1:T(1,128)} %fusion.220) | copy-start | bytes 192004
  113.1 1.2 copy-start.103
  115.5 1.2 copy-start.40
  116.7 1.0 copy-start.94
  126.7 2.4 copy-start.93
  135.3 1.2 copy-start.51
  138.5 1.0 copy-start.85
  138.5 1.0 copy-start.84
  138.5 1.9 copy-start.72
  138.5 2.5 copy-start.7
  140.3 17.4 %copy-start.17 = (f32[1,1,25,32]{2,3,1,0:T(8,128)}, f32[1,1,25,32]{2,3,1,0:T(8,128)S(1)}, u32[]{:S(2)}) copy-start(f32[1,1,25,32]{2,3,1,0:T(8,128)S(1)} %copy.2908) | copy-start | bytes 9604
  140.4 17.3 %copy-start.19 = (f32[25,32]{0,1:T(8,128)}, f32[25,32]{0,1:T(8,128)S(1)}, u32[]{:S(2)}) copy-start(f32[25,32]{0,1:T(8,128)S(1)} %copy.2728) | copy-start | bytes 9604
  140.4 1.5 copy-start.6
  141.1 1.6 copy-start.5
  142.7 1.0 copy-start.81
  143.5 1.7 copy-start.69
  144.3 10.4 %copy-start.21 = (f32[1,1,25,32]{2,3,1,0:T(8,128)}, f32[1,1,25,32]{2,3,1,0:T(8,128)S(1)}, u32[]{:S(2)}) copy-start(f32[1,1,25,32]{2,3,1,0:T(8,128)S(1)} %copy.2895) | copy-start | bytes 9604
  144.4 10.3 %copy-start.23 = (f32[25,32]{0,1:T(8,128)}, f32[25,32]{0,1:T(8,128)S(1)}, u32[]{:S(2)}) copy-start(f32[25,32]{0,1:T(8,128)S(1)} %copy.2712) | copy-start | bytes 9604
  145.9 1.7 copy-start.63
  146.0 2.6 %copy-start.25 = (f32[1,1,25,32]{2,3,1,0:T(8,128)}, f32[1,1,25,32]{2,3,1,0:T(8,128)S(1)}, u32[]{:S(2)}) copy-start(f32[1,1,25,32]{2,3,1,0:T(8,128)S(1)} %copy.2882) | copy-start | bytes 9604
  146.2 2.4 copy-start.27
  147.7 0.9 copy-start.60
  150.0 1.0 copy-start.61
  151.9 2.0 copy-start.31
  152.5 2.3 copy-start.115
  153.8 0.9 copy-start.57
  153.8 1.6 copy-start.54
  154.7 1.8 copy-start.2
  156.7 0.9 copy-start.66
  156.7 0.9 copy-start.56
  156.8 2.3 copy-start.30
  159.0 0.9 copy-start.35
  159.0 0.9 copy-start.36
  159.0 1.0 copy-start.37
  160.0 0.9 copy-start.32
  160.0 0.9 copy-start.48
  166.2 12.4 %copy-start.126 = (s32[128]{0:T(128)S(1)}, s32[128]{0:T(128)}, u32[]{:S(2)}) copy-start(s32[128]{0:T(128)} %compare_select_fusion.3) | copy-start | bytes 1540
  166.2 12.4 %copy-start.127 = (s32[128]{0:T(128)S(1)}, s32[128]{0:T(128)}, u32[]{:S(2)}) copy-start(s32[128]{0:T(128)} %compare_select_fusion.4) | copy-start | bytes 1540
  166.2 13.0 %copy-start.75 = (pred[3,2,25,4]{3,2,1,0:T(8,128)(4,1)S(1)}, pred[3,2,25,4]{3,2,1,0:T(8,128)(4,1)}, u32[]{:S(2)}) copy-start(pred[3,2,25,4]{3,2,1,0:T(8,128)(4,1)} %compare_and_fusion.1) | copy-start | bytes 1804
  167.1 12.3 %copy-start.9 = (f32[5,25,128]{2,1,0:T(8,128)S(1)}, f32[5,25,128]{2,1,0:T(8,128)}, u32[]{:S(2)}) copy-start(f32[5,25,128]{2,1,0:T(8,128)} %copy-done.8) | copy-start | bytes 192004
  167.1 21.1 %all-to-all-start.3 = ((f32[32,1,160]{2,1,0:T(1,128)}), f32[32,1,160]{2,1,0:T(1,128)}, u32[]{:S(2)}, u32[]{:S(2)}) async-start(f32[32,1,160]{2,1,0:T(1,128)} %reshape.3687), calls=%async_computation.3 | async-start | bytes 65536 | tf_op jit(solution)/shard_map/all_to_all | solution.py:194
  181.6 0.9 copy-start.11
  182.5 0.9 copy-start.13
  188.2 15.9 %all-to-all-start = ((f32[32,1,375]{2,1,0:T(1,128)}), f32[32,1,375]{2,1,0:T(1,128)}, u32[]{:S(2)}, u32[]{:S(2)}) async-start(f32[32,1,375]{2,1,0:T(1,128)} %reshape.3689), calls=%async_computation | async-start | bytes 98304 | tf_op jit(solution)/shard_map/all_to_all | solution.py:207
  199.4 1.3 copy-start.101
  199.4 1.3 copy-start.98
  207.6 0.9 copy-start.74
  207.7 0.9 copy-start.16
  212.7 19.6 %all-to-all-start.1 = ((f32[32,1,375]{2,1,0:T(1,128)}), f32[32,1,375]{2,1,0:T(1,128)S(1)}, u32[]{:S(2)}, u32[]{:S(2)}) async-start(f32[32,1,375]{2,1,0:T(1,128)} %reshape.3691), calls=%async_computation.1 | async-start | bytes 98304 | tf_op jit(solution)/shard_map/all_to_all | solution.py:211
  222.8 0.9 copy-start.62
  233.4 1.0 copy-start.15
  234.7 0.9 copy-start.119
  236.8 0.9 copy-start.14
  238.0 0.9 copy-start.118
  240.4 0.9 copy-start.117
  242.8 0.9 copy-start.116
  245.0 0.9 copy-start.34
  247.0 0.9 copy-start.121
  249.4 0.9 copy-start.120
  250.6 1.1 copy-start.3
  252.3 1.0 copy-start.4
  (68 other events, 50.6 us)
where the time goes:
time: 258 us; the launch traced here: 255 us
  local copies, waits for them, and re-layouts  120 us (47%)
  other arithmetic  60 us (23%)
  starting transfers between devices  36.1 us (14%)
  matrix products  15.5 us (6%)
  waiting for transfers between devices  11 us (4%)
  loops' own time  10.8 us (4%)
    unnamed x296, local copies, waits for them, and re-layouts  47.7 us
    gather x48, local copies, waits for them, and re-layouts, one_block(): jnp.take(state, block_cells, axis=2).reshape(5, 5, 5, 5, block_width)  14.1 us
    and x16, other arithmetic, one_block(): jnp.take(state, block_cells, axis=2).reshape(5, 5, 5, 5, block_width)  12.3 us
    all_to_all x1, starting transfers between devices, body(): lax.all_to_all(lax.all_to_all(shaped, 'grid', split_axis=1, concat_axis=1...  11.6 us
    another operation x1, loops' own time, interpolate(): values = lax.map(one_block, jnp.arange(blocks, dtype=jnp.int32))  10.8 us
    reduce_sum x18, other arithmetic, euler_flux(): jnp.sum(momenta * momenta, axis=0)  10.1 us
    all_to_all x1, starting transfers between devices, body(): lax.all_to_all(remote_plus.reshape(3, 5, 25, part_count, capacity), 'dom'...  9.97 us
    dynamic_slice x16, local copies, waits for them, and re-layouts, interpolate(): values = lax.map(one_block, jnp.arange(blocks, dtype=jnp.int32))  9.94 us
  transfers between devices with their start and end apart: 4, of which 2 were waited for; matrix products, arithmetic and copies ran while one was open for 34% of the time, Pallas kernels for 0%

commit v1 on v0

--- a/solution.py
+++ b/solution.py
@@ -1,3 +1,4 @@
+import functools
 import math
 import jax
 import jax.numpy as jnp
@@ -8,6 +9,21 @@
 volume_forms = ("ia,vabce->vibce", "ib,vabce->vaice", "ic,vabce->vabie")
 face_forms = ("a,vabce->vbce", "b,vabce->vace", "c,vabce->vabe")
 lift_forms = ("i,vbce->vibce", "i,vace->vaice", "i,vabe->vabie")
+
+
+def _draft_bench(xs, group_axis):
+    return jnp.concatenate(
+        lax.all_to_all(
+            jnp.stack(jnp.split(xs, lax.psum(1, axis_name=group_axis), axis=3)),
+            group_axis,
+            split_axis=0,
+            concat_axis=0,
+        ),
+        axis=3,
+    )
+
+
+see_blocks_for = functools.partial(_draft_bench, group_axis="dom")
 
 
 def gauss_nodes():
@@ -208,13 +224,7 @@
         3, 5, 25, remote
     )
     remote_plus = remote_fluxes(own_high, partner_low)
-    returned = lax.all_to_all(
-        remote_plus.reshape(3, 5, 25, part_count, capacity),
-        "dom",
-        split_axis=3,
-        concat_axis=3,
-        tiled=True,
-    )
+    returned = see_blocks_for(remote_plus.reshape(3, 5, 25, part_count, capacity))
     remote_minus = returned.reshape(3, 5, 25, remote)
     plus_common, minus_common = assemble(
         high_slots, low_slots, remote_plus, remote_minus, fringe, plus_order, minus_order

time: 258 us -> 259 us (level)
    unnamed x296 -> x326, local copies, waits for them, and re-layouts: 47.7 us -> 46.9 us
where the time goes in v1:
time: 259 us; the launch traced here: 256 us
  local copies, waits for them, and re-layouts  119 us (46%)
  other arithmetic  60.2 us (23%)
  starting transfers between devices  36.1 us (14%)
  matrix products  15.5 us (6%)
  waiting for transfers between devices  11.5 us (4%)
  loops' own time  11.1 us (4%)
    unnamed x326, local copies, waits for them, and re-layouts  46.9 us
    gather x48, local copies, waits for them, and re-layouts, one_block(): jnp.take(state, block_cells, axis=2).reshape(5, 5, 5, 5, block_width)  14.2 us
    and x16, other arithmetic, one_block(): jnp.take(state, block_cells, axis=2).reshape(5, 5, 5, 5, block_width)  12.3 us
    all_to_all x1, starting transfers between devices, body(): lax.all_to_all(lax.all_to_all(shaped, 'grid', split_axis=1, concat_axis=1...  11.6 us
    another operation x1, loops' own time, interpolate(): values = lax.map(one_block, jnp.arange(blocks, dtype=jnp.int32))  11.1 us
    reduce_sum x18, other arithmetic, euler_flux(): jnp.sum(momenta * momenta, axis=0)  10.2 us
    all_to_all x1, starting transfers between devices, _draft_bench(): lax.all_to_all(jnp.stack(jnp.split(xs, lax.psum(1, axis_name=group_axis),...  9.97 us
    dynamic_slice x16, local copies, waits for them, and re-layouts, interpolate(): values = lax.map(one_block, jnp.arange(blocks, dtype=jnp.int32))  9.75 us
  transfers between devices with their start and end apart: 4, of which 2 were waited for; matrix products, arithmetic and copies ran while one was open for 34% of the time, Pallas kernels for 0%

profile of v1, /device:TPU:8, one launch (start us, length us, event | category | flops | bytes accessed | tf_op | source)
XLA Modules:
  0.0 255.6 jit_solution(17516464295910704336)
XLA Ops:
  0.0 1.2 copy.3082
  1.3 58.3 %while.10 = (s32[]{:T(128)}, f32[16,5,64]{2,1,0:T(8,128)S(1)}, s32[16]{0:T(128)S(1)}, s32[1024]{0:T(1024)}, f32[5,125,128]{1,0,2:T(8,128)S(1)}, /*index=5*/f32[3...) while((s32[]{:T(128)}, f32[16,5,64]{2,1,0:T(8,128)S(1)}, ...), condition=%wide.region_8.10_spmd, body=%wide.region_7.9_spmd.sunk | while | flops 130696 | bytes 1246307 | solution.py:148
  60.6 9.6 %all-to-all-start.2 = ((f32[16,1,320]{2,1,0:T(1,128)}), f32[16,1,320]{2,1,0:T(1,128)}, u32[]{:S(2)}, u32[]{:S(2)}) async-start(f32[16,1,320]{2,1,0:T(1,128)} %reshape.3688), calls=%async_computation.2 | async-start | bytes 49152 | tf_op jit(solution)/shard_map/all_to_all | solution.py:211
  76.2 0.8 fusion.35
  79.0 1.2 fusion.219
  84.1 1.2 fusion.220
  95.4 1.0 scatter_custom_fusion
  98.5 0.9 fusion.36
  102.5 1.0 scatter_custom_fusion.3
  104.6 1.0 scatter_custom_fusion.2
  106.8 1.2 scatter_custom_fusion.1
  112.0 1.2 fusion.223
  113.2 1.2 fusion.20
  114.4 1.2 fusion.18
  115.6 1.2 fusion.224
  116.8 1.0 copy.3184
  118.4 2.5 gather_fusion.5
  121.5 1.9 fusion.39
  126.2 1.2 scatter_custom_fusion.5
  128.5 1.4 fusion.22
  129.9 1.4 fusion.16
  131.3 1.2 fusion.12
  132.5 1.1 scatter_custom_fusion.4
  134.7 1.2 fusion.14
  149.1 0.8 copy-done.60
  154.0 0.9 copy-done.57
  156.9 0.8 copy-done.66
  159.2 1.8 fusion.32
  161.0 0.9 copy-done.33
  164.6 1.5 reduce.22
  166.4 0.8 reshape.3690
  167.2 11.6 %all-to-all-start.3 = ((f32[32,1,160]{2,1,0:T(1,128)}), f32[32,1,160]{2,1,0:T(1,128)}, u32[]{:S(2)}, u32[]{:S(2)}) async-start(f32[32,1,160]{2,1,0:T(1,128)} %reshape.3690), calls=%async_computation.3 | async-start | bytes 65536 | tf_op jit(solution)/shard_map/all_to_all | solution.py:210
  180.4 1.3 reduce.24
  183.6 4.7 %all-to-all-done.3 = f32[32,1,160]{2,1,0:T(1,128)} async-done(((f32[32,1,160]{2,1,0:T(1,128)}), f32[32,1,160]{2,1,0:T(1,128)}, u32[]{:S(2)}, u32[]{:S(2)}) %all-to-all-start.3) | async-done | bytes 20512 | tf_op jit(solution)/shard_map/all_to_all | solution.py:210
  188.3 5.0 %all-to-all-start = ((f32[32,1,375]{2,1,0:T(1,128)}), f32[32,1,375]{2,1,0:T(1,128)}, u32[]{:S(2)}, u32[]{:S(2)}) async-start(f32[32,1,375]{2,1,0:T(1,128)} %reshape.3692), calls=%async_computation | async-start | bytes 98304 | tf_op jit(solution)/shard_map/all_to_all | solution.py:223
  193.3 1.5 reduce.23
  194.8 0.8 reshape.3691
  195.6 1.7 copy.3087
  197.4 2.3 gather_fusion.1
  199.6 1.2 copy.3089
  204.3 1.6 reduce.25
  208.8 0.9 copy-done.71
  209.7 0.9 copy-done.65
  211.4 1.3 reduce.26
  212.7 0.8 reshape.3694
  213.6 10.0 %all-to-all-start.1 = ((f32[32,1,375]{2,1,0:T(1,128)}), f32[32,1,375]{2,1,0:T(1,128)S(1)}, u32[]{:S(2)}, u32[]{:S(2)}) async-start(f32[32,1,375]{2,1,0:T(1,128)} %reshape.3694), calls=%async_computation.1 | async-start | bytes 98304 | tf_op jit(solution)/shard_map/all_to_all | solution.py:16
  223.7 0.8 copy-done.62
  224.5 0.9 copy-done.59
  225.4 0.9 copy-done.68
  226.3 6.9 %all-to-all-done.1 = f32[32,1,375]{2,1,0:T(1,128)S(1)} async-done(((f32[32,1,375]{2,1,0:T(1,128)}), f32[32,1,375]{2,1,0:T(1,128)S(1)}, u32[]{:S(2)}, u32[]{:S(2)}) %all-to-all-start.1) | async-done | bytes 48032 | tf_op jit(solution)/shard_map/all_to_all | solution.py:16
  235.7 0.9 gather_fusion.8
  237.1 0.8 copy-done.46
  239.2 0.9 gather_fusion.11
  240.5 0.8 copy-done.45
  241.6 0.9 gather_fusion.10
  242.9 0.8 copy-done.44
  244.0 0.9 gather_fusion.9
  245.3 0.8 copy-done.42
  246.1 0.8 copy-done.34
  247.4 0.9 gather_fusion.13
  248.7 0.8 copy-done.43
  249.8 0.9 gather_fusion.12
  251.1 0.8 copy-done.41
  253.9 0.9 fusion.6
  (856 shorter events, 131.0 us)
Async XLA Ops:
  0.0 1.2 copy-start.91
  59.5 10.7 %copy-start = (f32[5,125,128]{2,1,0:T(8,128)S(1)}, f32[5,125,128]{2,1,0:T(8,128)}, u32[]{:S(2)}) copy-start(f32[5,125,128]{2,1,0:T(8,128)} %param.18) | copy-start | bytes 960004
  60.6 103.4 %all-to-all-start.2 = ((f32[16,1,320]{2,1,0:T(1,128)}), f32[16,1,320]{2,1,0:T(1,128)}, u32[]{:S(2)}, u32[]{:S(2)}) async-start(f32[16,1,320]{2,1,0:T(1,128)} %reshape.3688), calls=%async_computation.2 | async-start | bytes 49152 | tf_op jit(solution)/shard_map/all_to_all | solution.py:211
  93.1 4.4 %copy-start.40 = (f32[1,5,25,128]{3,0,2,1:T(1,128)S(1)}, f32[1,5,25,128]{3,0,2,1:T(1,128)}, u32[]{:S(2)}) copy-start(f32[1,5,25,128]{3,0,2,1:T(1,128)} %fusion.219) | copy-start | bytes 192004
  113.2 1.2 copy-start.102
  115.6 1.2 copy-start.39
  116.8 1.0 copy-start.93
  126.2 2.3 copy-start.92
  134.7 1.2 copy-start.51
  137.8 1.9 copy-start.30
  139.8 1.4 copy-start.86
  139.8 1.5 copy-start.85
  139.8 1.6 copy-start.84
  139.8 1.6 copy-start.83
  140.4 2.6 %copy-start.7 = (f32[1,5,25,128]{2,3,1,0:T(8,128)S(1)}, f32[1,5,25,128]{2,3,1,0:T(8,128)}, u32[]{:S(2)}) copy-start(f32[1,5,25,128]{2,3,1,0:T(8,128)} %get-tuple-element.210) | copy-start | bytes 192004
  142.2 15.7 %copy-start.17 = (f32[1,1,25,32]{2,3,1,0:T(8,128)}, f32[1,1,25,32]{2,3,1,0:T(8,128)S(1)}, u32[]{:S(2)}) copy-start(f32[1,1,25,32]{2,3,1,0:T(8,128)S(1)} %copy.3248) | copy-start | bytes 9604
  142.3 15.6 %copy-start.19 = (f32[25,32]{0,1:T(8,128)}, f32[25,32]{0,1:T(8,128)S(1)}, u32[]{:S(2)}) copy-start(f32[25,32]{0,1:T(8,128)S(1)} %copy.3070) | copy-start | bytes 9604
  142.3 1.0 copy-start.6
  143.0 1.1 copy-start.5
  144.1 1.0 copy-start.80
  144.8 1.7 copy-start.69
  145.7 9.1 %copy-start.21 = (f32[1,1,25,32]{2,3,1,0:T(8,128)}, f32[1,1,25,32]{2,3,1,0:T(8,128)S(1)}, u32[]{:S(2)}) copy-start(f32[1,1,25,32]{2,3,1,0:T(8,128)S(1)} %copy.3235) | copy-start | bytes 9604
  145.8 9.1 %copy-start.23 = (f32[25,32]{0,1:T(8,128)}, f32[25,32]{0,1:T(8,128)S(1)}, u32[]{:S(2)}) copy-start(f32[25,32]{0,1:T(8,128)S(1)} %copy.3054) | copy-start | bytes 9604
  146.6 0.9 copy-start.88
  147.3 1.7 copy-start.63
  147.4 2.6 %copy-start.25 = (f32[1,1,25,32]{2,3,1,0:T(8,128)}, f32[1,1,25,32]{2,3,1,0:T(8,128)S(1)}, u32[]{:S(2)}) copy-start(f32[1,1,25,32]{2,3,1,0:T(8,128)S(1)} %copy.3222) | copy-start | bytes 9604
  147.6 2.4 copy-start.27
  149.1 0.9 copy-start.60
  151.4 1.0 copy-start.61
  153.3 1.6 copy-start.114
  153.9 1.6 copy-start.54
  154.8 1.8 copy-start.2
  156.9 0.9 copy-start.66
  156.9 0.9 copy-start.56
  156.9 2.2 copy-start.31
  157.9 1.3 copy-start.47
  159.2 1.8 copy-start.35
  159.2 1.8 copy-start.36
  161.0 0.9 copy-start.33
  161.0 0.9 copy-start.48
  166.3 12.4 %copy-start.125 = (s32[128]{0:T(128)S(1)}, s32[128]{0:T(128)}, u32[]{:S(2)}) copy-start(s32[128]{0:T(128)} %compare_select_fusion.3) | copy-start | bytes 1540
  166.3 12.4 %copy-start.126 = (s32[128]{0:T(128)S(1)}, s32[128]{0:T(128)}, u32[]{:S(2)}) copy-start(s32[128]{0:T(128)} %compare_select_fusion.4) | copy-start | bytes 1540
  166.4 13.0 %copy-start.74 = (pred[3,2,25,4]{3,2,1,0:T(8,128)(4,1)S(1)}, pred[3,2,25,4]{3,2,1,0:T(8,128)(4,1)}, u32[]{:S(2)}) copy-start(pred[3,2,25,4]{3,2,1,0:T(8,128)(4,1)} %compare_and_fusion.1) | copy-start | bytes 1804
  167.2 12.3 %copy-start.9 = (f32[5,25,128]{2,1,0:T(8,128)S(1)}, f32[5,25,128]{2,1,0:T(8,128)}, u32[]{:S(2)}) copy-start(f32[5,25,128]{2,1,0:T(8,128)} %copy-done.8) | copy-start | bytes 192004
  167.2 21.1 %all-to-all-start.3 = ((f32[32,1,160]{2,1,0:T(1,128)}), f32[32,1,160]{2,1,0:T(1,128)}, u32[]{:S(2)}, u32[]{:S(2)}) async-start(f32[32,1,160]{2,1,0:T(1,128)} %reshape.3690), calls=%async_computation.3 | async-start | bytes 65536 | tf_op jit(solution)/shard_map/all_to_all | solution.py:210
  181.8 0.9 copy-start.11
  188.3 16.0 %all-to-all-start = ((f32[32,1,375]{2,1,0:T(1,128)}), f32[32,1,375]{2,1,0:T(1,128)}, u32[]{:S(2)}, u32[]{:S(2)}) async-start(f32[32,1,375]{2,1,0:T(1,128)} %reshape.3692), calls=%async_computation | async-start | bytes 98304 | tf_op jit(solution)/shard_map/all_to_all | solution.py:223
  199.6 1.3 copy-start.100
  199.6 1.3 copy-start.97
  207.9 0.9 copy-start.73
  207.9 0.9 copy-start.16
  213.6 19.6 %all-to-all-start.1 = ((f32[32,1,375]{2,1,0:T(1,128)}), f32[32,1,375]{2,1,0:T(1,128)S(1)}, u32[]{:S(2)}, u32[]{:S(2)}) async-start(f32[32,1,375]{2,1,0:T(1,128)} %reshape.3694), calls=%async_computation.1 | async-start | bytes 98304 | tf_op jit(solution)/shard_map/all_to_all | solution.py:16
  223.6 0.9 copy-start.62
  234.5 1.0 copy-start.15
  235.7 0.9 copy-start.118
  237.9 1.0 copy-start.14
  239.1 0.9 copy-start.117
  241.5 0.9 copy-start.116
  243.9 0.9 copy-start.115
  247.4 0.9 copy-start.120
  249.8 0.9 copy-start.119
  250.9 1.1 copy-start.3
  251.9 0.9 copy-start.29
  252.8 1.0 copy-start.4
  (67 other events, 50.0 us)
